TPU v7x, 32 devices: a whole 2x2x4 slice. The times are simulated.
32 devices in a mesh: dp: 4 (over z), head: 2 (over x), width: 4 (over y, core).
Axes of the slice: x: 2, y: 2, z: 4, core: 2. Of those that a mesh axis runs over, the one named last changes fastest.
Arguments:
- block_in: bfloat16 [4096, 768], P('dp', ('head', 'width')), may hold values from -6 to 6
- segments: int32 [4096], P(('dp', 'head')), may hold values from 0 to 512, as said below
- live_counts: int32 [8], P('dp'), may hold values from 256 to 512, as said below
- norm1_gain: float32 [768], P(('head', 'width')), may hold values from 0.5 to 1.5
- norm1_bias: float32 [768], P(('head', 'width')), may hold values from -3 to 3
- qkv_weight: bfloat16 [768, 3, 768], P('head', None, 'width'), may hold values from -8 to 8
- qv_bias: float32 [2, 768], P(None, 'width'), may hold values from -4 to 4
- out_weight: bfloat16 [768, 768], P('width', 'head'), may hold values from -1 to 1
- out_bias: float32 [768], P(('head', 'width')), may hold values from -4 to 4
- norm2_gain: float32 [768], P(('head', 'width')), may hold values from 0.5 to 1.5
- norm2_bias: float32 [768], P(('head', 'width')), may hold values from -3 to 3
- up_weight: bfloat16 [768, 3072], P('head', 'width'), may hold values from -0.21875 to 0.21875
- up_bias: float32 [3072], P('width'), may hold values from -4 to 4
- down_weight: bfloat16 [3072, 768], P('width', 'head'), may hold values from -0.109375 to 0.109375
- down_bias: float32 [768], P(('head', 'width')), may hold values from -4 to 4
- out_cot: bfloat16 [4096, 768], P('dp', ('head', 'width')), may hold values from -6 to 6
Outputs:
- block_out: bfloat16 [4096, 768], P('dp', ('head', 'width'))
- grad_in: float32 [4096, 768], P('dp', ('head', 'width'))
- grad_norm1_gain: float32 [768], P(('head', 'width'))
- grad_norm1_bias: float32 [768], P(('head', 'width'))
- grad_qkv_weight: float32 [768, 3, 768], P('head', None, 'width')
- grad_qv_bias: float32 [2, 768], P(None, 'width')
- grad_out_weight: float32 [768, 768], P('width', 'head')
- grad_out_bias: float32 [768], P(('head', 'width'))
- grad_norm2_gain: float32 [768], P(('head', 'width'))
- grad_norm2_bias: float32 [768], P(('head', 'width'))
- grad_up_weight: float32 [768, 3072], P('head', 'width')
- grad_up_bias: float32 [3072], P('width')
- grad_down_weight: float32 [3072, 768], P('width', 'head')
- grad_down_bias: float32 [768], P(('head', 'width'))
Inputs may be any that keep to these rules, and one draw needn't show every extreme that they name: `segments`: within a token block the document numbers never fall; live slots come first and carry numbers from 0 up; every slot at or past the block's live count carries 512. `live_counts`: live slots of a token block; some block is full and some holds exactly 256.
All inputs are finite; a program needn't handle non-finite values.
Results may differ from a plain program's by a relative error of at most 0.013.
Values may be sent and summed in bfloat16 or wider, within the bound.
No kernel may reach another device: no remote copies, remote signals or barrier semaphores. Data moves between devices by JAX's collectives and lax.ppermute only.
A program may use at most 64 MiB of HBM per device.

v0:
```python
import jax
import jax.numpy as jnp
from jax import lax
from jax.sharding import PartitionSpec as P

D = 768
HD = 64
norm_eps = 1e-05


def gelu_fn(values):
    return jax.nn.gelu(values, approximate=True)


def moments(first_stat, second_stat):
    return lax.psum((first_stat, second_stat), ("head", "width"))


def widen_rows(narrow_rows):
    return lax.all_gather(narrow_rows, "width", axis=1, tiled=True)


def narrow_sum(partial_rows):
    return lax.psum_scatter(partial_rows, "width", scatter_dimension=1, tiled=True)


def hidden_whole(half_rows):
    return lax.all_gather(half_rows, "head", axis=0, tiled=True)


def norm_forward(rows_f, gain, shift):
    row_sums, row_squares = moments(jnp.sum(rows_f, axis=1), jnp.sum(rows_f * rows_f, axis=1))
    row_mean = row_sums / D
    row_var = row_squares / D - row_mean * row_mean
    inv_std = lax.rsqrt(row_var + norm_eps)[:, None]
    normed = (rows_f - row_mean[:, None]) * inv_std
    return (normed, inv_std, (normed * gain + shift).astype(jnp.bfloat16))


def norm_backward(grad_n, normed, inv_std, gain):
    scaled = grad_n * gain
    first_sum, second_sum = moments(jnp.sum(scaled, axis=1), jnp.sum(scaled * normed, axis=1))
    return inv_std * (scaled - first_sum[:, None] / D - normed * (second_sum[:, None] / D))


def body(
    block_in,
    segments,
    live_counts,
    norm1_gain,
    norm1_bias,
    qkv_weight,
    qv_bias,
    out_weight,
    out_bias,
    norm2_gain,
    norm2_bias,
    up_weight,
    up_bias,
    down_weight,
    down_bias,
    out_cot,
):
    group_rows = block_in.shape[0]
    slot_count = segments.shape[0]
    head_cols = qkv_weight.shape[2]
    local_heads = head_cols // HD
    scale_factor = HD ** (-0.5)
    qkv_flat = qkv_weight.reshape(qkv_weight.shape[0], 3 * head_cols)
    rows_f = block_in.astype(jnp.float32)
    normed1, inv1, n1_b = norm_forward(rows_f, norm1_gain, norm1_bias)
    n1_wide = widen_rows(n1_b)
    picked = n1_wide
    qkv_f = lax.psum_scatter(
        jnp.dot(picked, qkv_flat, preferred_element_type=jnp.float32),
        "head",
        scatter_dimension=0,
        tiled=True,
    )
    qkv_f = qkv_f.reshape(slot_count, 3, head_cols)
    queries = (qkv_f[:, 0] + qv_bias[0]).astype(jnp.bfloat16).reshape(slot_count, local_heads, HD)
    key_rows = qkv_f[:, 1].astype(jnp.bfloat16).reshape(slot_count, local_heads, HD)
    values = (qkv_f[:, 2] + qv_bias[1]).astype(jnp.bfloat16).reshape(slot_count, local_heads, HD)
    slot_pos = jnp.arange(slot_count)
    allowed = (segments[:, None] == segments[None, :]) & (slot_pos[None, :] <= slot_pos[:, None])

    def masked_scores():
        raw = (
            jnp.einsum("qhd,khd->hqk", queries, key_rows, preferred_element_type=jnp.float32)
            * scale_factor
        )
        return jnp.where(allowed[None], raw, -1e30)

    scores = masked_scores()
    peak = jnp.max(scores, axis=-1, keepdims=True)
    log_total = peak + jnp.log(jnp.sum(jnp.exp(scores - peak), axis=-1, keepdims=True))
    probs_b = jnp.exp(scores - log_total).astype(jnp.bfloat16)
    mixed = jnp.einsum("hqk,khd->qhd", probs_b, values, preferred_element_type=jnp.float32).astype(
        jnp.bfloat16
    )
    mixed_flat = mixed.reshape(slot_count, head_cols)
    mixed_all = lax.all_gather(mixed_flat, "head", axis=0, tiled=True)
    resid1 = (
        rows_f
        + narrow_sum(jnp.dot(mixed_all, out_weight, preferred_element_type=jnp.float32))
        + out_bias
    )
    normed2, inv2, n2_b = norm_forward(resid1, norm2_gain, norm2_bias)
    n2_wide = widen_rows(n2_b)
    picked = n2_wide
    pre_act = (
        lax.psum_scatter(
            jnp.dot(picked, up_weight, preferred_element_type=jnp.float32),
            "head",
            scatter_dimension=0,
            tiled=True,
        )
        + up_bias
    )
    hidden = gelu_fn(pre_act).astype(jnp.bfloat16)
    hidden_all = hidden_whole(hidden)
    result = (
        resid1
        + narrow_sum(jnp.dot(hidden_all, down_weight, preferred_element_type=jnp.float32))
        + down_bias
    )
    block_out = result.astype(jnp.bfloat16)
    row_ids = jnp.arange(group_rows)
    owner = row_ids // slot_count
    own_count = jnp.sum(
        jnp.where(
            owner[:, None] == jnp.arange(live_counts.shape[0])[None, :], live_counts[None, :], 0
        ),
        axis=1,
    )
    live = (row_ids % slot_count < own_count)[:, None]
    grad_out = jnp.where(live, out_cot.astype(jnp.float32), 0.0)
    grad_out_wide = widen_rows(grad_out.astype(jnp.bfloat16))
    g_down_w = jnp.einsum(
        "tf,td->fd", hidden_all, grad_out_wide, preferred_element_type=jnp.float32
    )
    g_down_b = jnp.sum(grad_out, axis=0)
    picked = grad_out_wide
    grad_hidden = lax.psum_scatter(
        jnp.einsum("td,fd->tf", picked, down_weight, preferred_element_type=jnp.float32),
        "head",
        scatter_dimension=0,
        tiled=True,
    )
    _, pull_back = jax.vjp(gelu_fn, pre_act)
    grad_pre_b = pull_back(grad_hidden)[0].astype(jnp.bfloat16)
    grad_pre_all = hidden_whole(grad_pre_b)
    g_up_w = jnp.einsum("tc,tf->cf", n2_wide, grad_pre_all, preferred_element_type=jnp.float32)
    g_up_b = jnp.sum(grad_pre_all.astype(jnp.float32), axis=0)
    grad_n2 = narrow_sum(
        jnp.einsum("tf,cf->tc", grad_pre_all, up_weight, preferred_element_type=jnp.float32)
    )
    g_norm2_gain = jnp.sum(grad_n2 * normed2, axis=0)
    g_norm2_bias = jnp.sum(grad_n2, axis=0)
    grad_x1 = grad_out + norm_backward(grad_n2, normed2, inv2, norm2_gain)
    grad_x1_wide = widen_rows(grad_x1.astype(jnp.bfloat16))
    g_out_w = jnp.einsum("tc,td->cd", mixed_all, grad_x1_wide, preferred_element_type=jnp.float32)
    g_out_b = jnp.sum(grad_x1, axis=0)
    picked = grad_x1_wide
    grad_mix = lax.psum_scatter(
        jnp.einsum("td,cd->tc", picked, out_weight, preferred_element_type=jnp.float32),
        "head",
        scatter_dimension=0,
        tiled=True,
    )
    grad_mix = grad_mix.reshape(slot_count, local_heads, HD)
    grad_mix_b = grad_mix.astype(jnp.bfloat16)
    delta = jnp.sum(grad_mix * mixed.astype(jnp.float32), axis=-1).T[:, :, None]
    probs_f = jnp.exp(masked_scores() - log_total)
    probs_again = probs_f.astype(jnp.bfloat16)
    grad_probs = jnp.einsum("qhd,khd->hqk", grad_mix_b, values, preferred_element_type=jnp.float32)
    grad_scores = (probs_f * (grad_probs - delta)).astype(jnp.bfloat16)
    grad_q = (
        jnp.einsum("hqk,khd->qhd", grad_scores, key_rows, preferred_element_type=jnp.float32)
        * scale_factor
    )
    grad_k = (
        jnp.einsum("hqk,qhd->khd", grad_scores, queries, preferred_element_type=jnp.float32)
        * scale_factor
    )
    grad_v = jnp.einsum("hqk,qhd->khd", probs_again, grad_mix_b, preferred_element_type=jnp.float32)
    grad_qkv = (
        jnp.stack([grad_q, grad_k, grad_v], axis=1)
        .reshape(slot_count, 3 * head_cols)
        .astype(jnp.bfloat16)
    )
    grad_qkv_all = lax.all_gather(grad_qkv, "head", axis=0, tiled=True)
    g_qkv_w = jnp.einsum(
        "tc,tf->cf", n1_wide, grad_qkv_all, preferred_element_type=jnp.float32
    ).reshape(qkv_weight.shape)
    column_sums = jnp.sum(grad_qkv_all.astype(jnp.float32), axis=0).reshape(3, head_cols)
    g_qv_b = jnp.stack([column_sums[0], column_sums[2]], axis=0)
    grad_n1 = narrow_sum(
        jnp.einsum("tf,cf->tc", grad_qkv_all, qkv_flat, preferred_element_type=jnp.float32)
    )
    g_norm1_gain = jnp.sum(grad_n1 * normed1, axis=0)
    g_norm1_bias = jnp.sum(grad_n1, axis=0)
    grad_in = grad_x1 + norm_backward(grad_n1, normed1, inv1, norm1_gain)
    summed = lax.psum(
        (
            g_norm1_gain,
            g_norm1_bias,
            g_qkv_w,
            g_qv_b,
            g_out_w,
            g_out_b,
            g_norm2_gain,
            g_norm2_bias,
            g_up_w,
            g_up_b,
            g_down_w,
            g_down_b,
        ),
        "dp",
    )
    return (block_out, grad_in) + tuple(summed)


def solution(mesh):
    return jax.shard_map(
        body,
        mesh=mesh,
        in_specs=(
            P("dp", ("head", "width")),
            P(("dp", "head")),
            P("dp"),
            P(("head", "width")),
            P(("head", "width")),
            P("head", None, "width"),
            P(None, "width"),
            P("width", "head"),
            P(("head", "width")),
            P(("head", "width")),
            P(("head", "width")),
            P("head", "width"),
            P("width"),
            P("width", "head"),
            P(("head", "width")),
            P("dp", ("head", "width")),
        ),
        out_specs=(
            P("dp", ("head", "width")),
            P("dp", ("head", "width")),
            P(("head", "width")),
            P(("head", "width")),
            P("head", None, "width"),
            P(None, "width"),
            P("width", "head"),
            P(("head", "width")),
            P(("head", "width")),
            P(("head", "width")),
            P("head", "width"),
            P("width"),
            P("width", "head"),
            P(("head", "width")),
        ),
        check_vma=False,
    )
```

profile of v0, /device:TPU:0, one launch (start us, length us, event | category | flops | bytes accessed | tf_op | source)
XLA Modules:
  0.0 568.9 jit_solution(2139136913742872445)
XLA Ops:
  8.3 15.4 %all-reduce.3 = (f32[1024]{0:T(1024)S(1)}, f32[1024]{0:T(1024)S(1)}) all-reduce(f32[1024]{0:T(1024)S(1)} %get-tuple-element.25, f32[1024]{0:T(1024)S(1)} %get-tuple-element.24), channel_id=1, replica_groups=mesh['dp'=4,'head'=2,'width'=4] {'head','width'}, use_global_device_ids=true, to_apply=%region_3.0 | all-reduce | flops 2048 | bytes 16384 | tf_op jit(solution)/shard_map/psum | solution.py:16
  24.9 7.2 %all_gather.24 = bf16[1024,384]{0,1:T(8,128)(2,1)S(1)} all-gather(bf16[1024,96]{0,1:T(8,128)(2,1)S(1)} %fusion.21), channel_id=1, replica_groups=mesh['dp'=4,'head'=2,'width'=4] {'width'}, dimensions={1}, use_global_device_ids=true | all-gather | bytes 983040 | tf_op jit(solution)/shard_map/all_gather | solution.py:20
  36.3 34.6 %reduce-scatter.9.cloned.1.call-done = f32[512,576]{0,1:T(8,128)} async-done(((f32[1024,576]{0,1:T(8,128)}), f32[512,576]{0,1:T(8,128)}) %reduce-scatter.9.cloned.1.call-update) | async-done | bytes 1179664 | tf_op jit(solution)/shard_map/reduce_scatter | solution.py:74
  76.7 7.1 %all_gather.25 = bf16[1024,192]{0,1:T(8,128)(2,1)S(1)} all-gather(bf16[512,192]{0,1:T(8,128)(2,1)S(1)} %bitcast.65), channel_id=1, replica_groups=mesh['dp'=4,'head'=2,'width'=4] {'head'}, dimensions={0}, use_global_device_ids=true | all-gather | bytes 589824 | tf_op jit(solution)/shard_map/all_gather | solution.py:102
  85.7 8.6 %all_gather.28 = bf16[1024,384]{0,1:T(8,128)(2,1)S(1)} all-gather(bf16[1024,96]{0,1:T(8,128)(2,1)S(1)} %fusion.30), channel_id=1, replica_groups=mesh['dp'=4,'head'=2,'width'=4] {'width'}, dimensions={1}, use_global_device_ids=true | all-gather | bytes 983040 | tf_op jit(solution)/shard_map/all_gather | solution.py:20
  94.3 2.7 fusion.51
  97.1 16.6 %reduce-scatter.11.cloned.1.call-done = f32[1024,96]{0,1:T(8,128)} async-done(((f32[1024,384]{0,1:T(8,128)}), f32[1024,96]{0,1:T(8,128)}) %reduce-scatter.11.cloned.1.call-update) | async-done | bytes 393232 | tf_op jit(solution)/shard_map/reduce_scatter | solution.py:24
  114.8 13.4 %all-reduce.2 = (f32[1024]{0:T(1024)S(1)}, f32[1024]{0:T(1024)S(1)}) all-reduce(f32[1024]{0:T(1024)S(1)} %get-tuple-element.23, f32[1024]{0:T(1024)S(1)} %get-tuple-element.22), channel_id=1, replica_groups=mesh['dp'=4,'head'=2,'width'=4] {'head','width'}, use_global_device_ids=true, to_apply=%region_11.12 | all-reduce | flops 2048 | bytes 16384 | tf_op jit(solution)/shard_map/psum | solution.py:16
  128.4 7.2 %all_gather.26 = bf16[1024,384]{0,1:T(8,128)(2,1)S(1)} all-gather(bf16[1024,96]{0,1:T(8,128)(2,1)S(1)} %add_convert_fusion.1), channel_id=1, replica_groups=mesh['dp'=4,'head'=2,'width'=4] {'width'}, dimensions={1}, use_global_device_ids=true | all-gather | bytes 983040 | tf_op jit(solution)/shard_map/all_gather | solution.py:20
  136.5 2.7 fusion.49
  139.3 20.2 %reduce-scatter.17.cloned.1.call-done = f32[512,768]{1,0:T(8,128)} async-done(((f32[1024,768]{1,0:T(8,128)}), f32[512,768]{1,0:T(8,128)}) %reduce-scatter.17.cloned.1.call-update) | async-done | bytes 1572880 | tf_op jit(solution)/shard_map/reduce_scatter | solution.py:144
  159.5 45.7 %reduce-scatter.13.cloned.1.call-done = f32[512,768]{1,0:T(8,128)} async-done(((f32[1024,768]{1,0:T(8,128)}), f32[512,768]{1,0:T(8,128)}) %reduce-scatter.13.cloned.1.call-update) | async-done | bytes 1572880 | tf_op jit(solution)/shard_map/reduce_scatter | solution.py:112
  205.1 4.2 fusion.8
  210.0 26.7 %all-gather.6.cloned.1.call-done = bf16[1024,768]{1,0:T(8,128)(2,1)} async-done(((bf16[512,768]{1,0:T(8,128)(2,1)}), bf16[1024,768]{1,0:T(8,128)(2,1)}) %all-gather.6.cloned.1.call-update) | async-done | bytes 1572880 | tf_op jit(solution)/shard_map/all_gather | solution.py:28
  236.7 3.4 fusion.52
  240.1 25.8 %all-gather.4.cloned.1.call-done = bf16[1024,768]{1,0:T(8,128)(2,1)} async-done(((bf16[512,768]{1,0:T(8,128)(2,1)}), bf16[1024,768]{1,0:T(8,128)(2,1)}) %all-gather.4.cloned.1.call-update) | async-done | bytes 1572880 | tf_op jit(solution)/shard_map/all_gather | solution.py:28
  265.9 3.6 fusion.50
  269.6 26.9 %reduce-scatter.19.cloned.1.call-done = f32[1024,96]{0,1:T(8,128)} async-done(((f32[1024,384]{0,1:T(8,128)}), f32[1024,96]{0,1:T(8,128)}) %reduce-scatter.19.cloned.1.call-update) | async-done | bytes 393232 | tf_op jit(solution)/shard_map/reduce_scatter | solution.py:24
  298.3 12.7 %all-reduce.1 = (f32[1024]{0:T(1024)S(1)}, f32[1024]{0:T(1024)S(1)}) all-reduce(f32[1024]{0:T(1024)S(1)} %get-tuple-element.15, f32[1024]{0:T(1024)S(1)} %get-tuple-element.19), channel_id=1, replica_groups=mesh['dp'=4,'head'=2,'width'=4] {'head','width'}, use_global_device_ids=true, to_apply=%region_20.21 | all-reduce | flops 2048 | bytes 16384 | tf_op jit(solution)/shard_map/psum | solution.py:16
  311.0 16.1 %reduce-scatter.15.cloned.1.call-done = f32[1024,96]{0,1:T(8,128)} async-done(((f32[1024,384]{0,1:T(8,128)}), f32[1024,96]{0,1:T(8,128)}) %reduce-scatter.15.cloned.1.call-update) | async-done | bytes 393232 | tf_op jit(solution)/shard_map/reduce_scatter | solution.py:24
  327.1 2.7 fusion.44
  329.8 8.0 %all_gather.30 = bf16[1024,384]{0,1:T(8,128)(2,1)S(1)} all-gather(bf16[1024,96]{0,1:T(8,128)(2,1)S(1)} %convert_element_type.83), channel_id=1, replica_groups=mesh['dp'=4,'head'=2,'width'=4] {'width'}, dimensions={1}, use_global_device_ids=true | all-gather | bytes 983040 | tf_op jit(solution)/shard_map/all_gather | solution.py:20
  339.3 17.9 %reduce-scatter.21.cloned.1.call-done = f32[512,192]{0,1:T(8,128)} async-done(((f32[1024,192]{0,1:T(8,128)}), f32[512,192]{0,1:T(8,128)}) %reduce-scatter.21.cloned.1.call-update) | async-done | bytes 393232 | tf_op jit(solution)/shard_map/reduce_scatter | solution.py:165
  358.4 3.1 fusion.11
  365.2 22.9 %all-gather.8.cloned.1.call-done = bf16[1024,576]{0,1:T(8,128)(2,1)} async-done(((bf16[512,576]{0,1:T(8,128)(2,1)}), bf16[1024,576]{0,1:T(8,128)(2,1)}) %all-gather.8.cloned.1.call-update) | async-done | bytes 1179664 | tf_op jit(solution)/shard_map/all_gather | solution.py:192
  388.1 3.3 fusion.53
  391.5 3.6 fusion.57
  401.9 17.7 %reduce-scatter.23.cloned.1.call-done = f32[1024,96]{0,1:T(8,128)} async-done(((f32[1024,384]{0,1:T(8,128)}), f32[1024,96]{0,1:T(8,128)}) %reduce-scatter.23.cloned.1.call-update) | async-done | bytes 393232 | tf_op jit(solution)/shard_map/reduce_scatter | solution.py:24
  421.0 13.0 %all-reduce.4 = (f32[96]{0:T(128)}, f32[96]{0:T(128)}, f32[2,192]{1,0:T(2,128)}, f32[96]{0:T(128)}, f32[96]{0:T(128)}, /*index=5*/f32[96]{0:T(128)}, f32[768]{0:T(1024)}, f32[96]{0:T(128)}) all-reduce(f32[96]{0:T(128)S(1)} %get-tuple-element.16, f32[96]{0:T(128)S(1)} %get-tuple-element.21, ...), channel_id=1, replica_groups=mesh['dp'=4,'head'=2,'width'=4] {'dp'}, use_global_device_ids=true, to_apply=%region_29.30 | all-reduce | flops 1728 | bytes 13824 | tf_op jit(solution)/shard_map/psum | solution.py:204
  434.0 12.8 %all-reduce = (f32[1024]{0:T(1024)S(1)}, f32[1024]{0:T(1024)S(1)}) all-reduce(f32[1024]{0:T(1024)S(1)} %get-tuple-element.17, f32[1024]{0:T(1024)S(1)} %get-tuple-element.18), channel_id=1, replica_groups=mesh['dp'=4,'head'=2,'width'=4] {'head','width'}, use_global_device_ids=true, to_apply=%region_27.28 | all-reduce | flops 2048 | bytes 16384 | tf_op jit(solution)/shard_map/psum | solution.py:16
  448.7 108.4 %all-reduce.8.cloned.1.call-done = (f32[384,3,192]{0,2,1:T(8,128)}, f32[192,384]{1,0:T(8,128)}, f32[384,768]{1,0:T(8,128)}, f32[768,384]{1,0:T(8,128)}) async-done(((f32[384,3,192]{0,2,1:T(8,128)}, f32[192,384]{1,0:T(8,128)}, f32[384,768]{1,0:T(8,128)}, f32[768,384]{1,0:T(8,128)}), (f32[384,3,192]{0,2,1:T(8,128)}, f32[192,384]{1,0:T(8,128)}, f32[384,768]{1,0:T(8,128)}, ...) | async-done | bytes 3538960 | tf_op jit(solution)/shard_map/psum | solution.py:204
  557.1 2.2 copy.49
  (165 shorter events, 37.6 us)
Async XLA Ops:
  7.2 129.3 %copy-start = (bf16[384,768]{1,0:T(8,128)(2,1)S(1)}, bf16[384,768]{1,0:T(8,128)(2,1)}, u32[]{:S(2)}) copy-start(bf16[384,768]{1,0:T(8,128)(2,1)} %param.27) | copy-start | bytes 1769476
  7.2 25.8 %copy-start.14 = (bf16[384,3,192]{0,2,1:T(8,128)(2,1)S(1)}, bf16[384,3,192]{0,2,1:T(8,128)(2,1)}, u32[]{:S(2)}) copy-start(bf16[384,3,192]{0,2,1:T(8,128)(2,1)} %param.21) | copy-start | bytes 1327108
  7.2 63.7 %reduce-scatter.9.cloned.1.call-start = ((), (), s32[]{:S(2)}) async-start(), calls=%async_computation.8 | async-start | bytes 3538944 | tf_op jit(solution)/shard_map/reduce_scatter | solution.py:74
  35.2 78.4 %reduce-scatter.11.cloned.1.call-start = ((), (), s32[]{:S(2)}) async-start(), calls=%async_computation.9 | async-start | bytes 1966080 | tf_op jit(solution)/shard_map/reduce_scatter | solution.py:24
  36.0 38.0 %copy-start.26 = (f32[3,64]{1,0:T(4,128)}, f32[3,64]{1,0:T(4,128)S(1)}, u32[]{:S(2)}) copy-start(f32[3,64]{1,0:T(4,128)S(1)} %add.174) | copy-start | bytes 2308
  36.1 38.7 %copy-start.37 = (f32[3,64]{1,0:T(4,128)}, f32[3,64]{1,0:T(4,128)S(1)}, u32[]{:S(2)}) copy-start(f32[3,64]{1,0:T(4,128)S(1)} %add.171) | copy-start | bytes 2308
  36.3 38.5 %copy-start.10 = (pred[512,512]{0,1:T(8,128)(4,1)}, pred[512,512]{0,1:T(8,128)(4,1)S(1)}, u32[]{:S(2)}) copy-start(pred[512,512]{0,1:T(8,128)(4,1)S(1)} %fusion.14) | copy-start | bytes 786436
  85.5 74.0 %reduce-scatter.17.cloned.1.call-start = ((), (), s32[]{:S(2)}) async-start(), calls=%async_computation.13 | async-start | bytes 4718592 | tf_op jit(solution)/shard_map/reduce_scatter | solution.py:144
  85.6 11.4 %copy-start.28 = (pred[1024]{0:T(1024)(128)(4,1)}, pred[1024]{0:T(1024)(128)(4,1)S(1)}, u32[]{:S(2)}) copy-start(pred[1024]{0:T(1024)(128)(4,1)S(1)} %fusion.35) | copy-start | bytes 3076
  97.0 16.7 %copy-start.3 = (bf16[1024,96]{0,1:T(8,128)(2,1)S(1)}, bf16[1024,96]{0,1:T(8,128)(2,1)}, u32[]{:S(2)}) copy-start(bf16[1024,96]{0,1:T(8,128)(2,1)} %param.16) | copy-start | bytes 589828
  97.0 16.7 %copy-start.44 = (f32[96]{0:T(128)S(1)}, f32[96]{0:T(128)}, u32[]{:S(2)}) copy-start(f32[96]{0:T(128)} %param.24) | copy-start | bytes 1156
  97.0 31.2 %copy-start.34 = (f32[96]{0:T(128)S(1)}, f32[96]{0:T(128)}, u32[]{:S(2)}) copy-start(f32[96]{0:T(128)} %param.25) | copy-start | bytes 1156
  97.0 31.2 %copy-start.45 = (f32[96]{0:T(128)S(1)}, f32[96]{0:T(128)}, u32[]{:S(2)}) copy-start(f32[96]{0:T(128)} %param.26) | copy-start | bytes 1156
  97.1 108.1 %reduce-scatter.13.cloned.1.call-start = ((), (), s32[]{:S(2)}) async-start(), calls=%async_computation.10 | async-start | bytes 4718592 | tf_op jit(solution)/shard_map/reduce_scatter | solution.py:112
  139.2 66.0 %copy-start.36 = (f32[768]{0:T(1024)S(1)}, f32[768]{0:T(1024)}, u32[]{:S(2)}) copy-start(f32[768]{0:T(1024)} %param.28) | copy-start | bytes 9220
  139.2 97.5 %all-gather.6.cloned.1.call-start = ((), (), s32[]{:S(2)}) async-start(), calls=%async_computation.14 | async-start | bytes 2359296 | tf_op jit(solution)/shard_map/all_gather | solution.py:28
  209.4 56.5 %all-gather.4.cloned.1.call-start = ((), (), s32[]{:S(2)}) async-start(), calls=%async_computation.11 | async-start | bytes 2359296 | tf_op jit(solution)/shard_map/all_gather | solution.py:28
  209.9 86.5 %reduce-scatter.19.cloned.1.call-start = ((), (), s32[]{:S(2)}) async-start(), calls=%async_computation.15 | async-start | bytes 1966080 | tf_op jit(solution)/shard_map/reduce_scatter | solution.py:24
  240.1 87.0 %reduce-scatter.15.cloned.1.call-start = ((), (), s32[]{:S(2)}) async-start(), calls=%async_computation.12 | async-start | bytes 1966080 | tf_op jit(solution)/shard_map/reduce_scatter | solution.py:24
  269.5 57.6 %copy-start.29 = (pred[1024]{0:T(1024)(128)(4,1)S(1)}, pred[1024]{0:T(1024)(128)(4,1)}, u32[]{:S(2)}) copy-start(pred[1024]{0:T(1024)(128)(4,1)} %copy-done.28) | copy-start | bytes 3076
  269.5 57.6 %copy-start.35 = (f32[96]{0:T(128)S(1)}, f32[96]{0:T(128)}, u32[]{:S(2)}) copy-start(f32[96]{0:T(128)} %param.25) | copy-start | bytes 1156
  269.5 57.6 %copy-start.47 = (f32[96]{0:T(128)S(1)}, f32[96]{0:T(128)}, u32[]{:S(2)}) copy-start(f32[96]{0:T(128)} %param.30) | copy-start | bytes 1156
  269.5 87.7 %reduce-scatter.21.cloned.1.call-start = ((), (), s32[]{:S(2)}) async-start(), calls=%async_computation.16 | async-start | bytes 1179648 | tf_op jit(solution)/shard_map/reduce_scatter | solution.py:165
  337.8 20.6 %copy-start.32 = (f32[3,512]{1,0:T(4,128)S(1)}, f32[3,512]{1,0:T(4,128)}, u32[]{:S(2)}) copy-start(f32[3,512]{1,0:T(4,128)} %copy-done.31) | copy-start | bytes 18436
  339.1 49.0 %all-gather.8.cloned.1.call-start = ((), (), s32[]{:S(2)}) async-start(), calls=%async_computation.17 | async-start | bytes 1769472 | tf_op jit(solution)/shard_map/all_gather | solution.py:192
  365.2 54.5 %reduce-scatter.23.cloned.1.call-start = ((), (), s32[]{:S(2)}) async-start(), calls=%async_computation.18 | async-start | bytes 1966080 | tf_op jit(solution)/shard_map/reduce_scatter | solution.py:24
  391.5 165.6 %all-reduce.8.cloned.1.call-start = ((), (), s32[]{:S(2)}) async-start(), calls=%async_computation.19 | async-start | bytes 7077888 | tf_op jit(solution)/shard_map/psum | solution.py:204
  399.8 19.8 %copy-start.33 = (f32[96]{0:T(128)S(1)}, f32[96]{0:T(128)}, u32[]{:S(2)}) copy-start(f32[96]{0:T(128)} %param.19) | copy-start | bytes 1156
  399.8 21.1 %copy-start.40 = (f32[96]{0:T(128)S(1)}, f32[96]{0:T(128)}, u32[]{:S(2)}) copy-start(f32[96]{0:T(128)} %get-tuple-element.14) | copy-start | bytes 1156
  399.8 21.1 %copy-start.41 = (f32[96]{0:T(128)S(1)}, f32[96]{0:T(128)}, u32[]{:S(2)}) copy-start(f32[96]{0:T(128)} %get-tuple-element.20) | copy-start | bytes 1156
  399.9 21.1 %copy-start.42 = (f32[96]{0:T(128)S(1)}, f32[96]{0:T(128)}, u32[]{:S(2)}) copy-start(f32[96]{0:T(128)} %get-tuple-element.48) | copy-start | bytes 1156
  399.9 21.1 %copy-start.43 = (f32[96]{0:T(128)S(1)}, f32[96]{0:T(128)}, u32[]{:S(2)}) copy-start(f32[96]{0:T(128)} %get-tuple-element.56) | copy-start | bytes 1156
  (28 other events, 88.9 us)
Sparse Core Ops, SparseCore 0:
  35.4 35.5 reduce-scatter.8
  85.6 28.0 reduce-scatter.10
  115.9 43.5 reduce-scatter.16
  161.6 43.5 reduce-scatter.12
  209.5 27.1 all-gather.5
  238.7 27.1 all-gather.3
  268.4 28.0 reduce-scatter.18
  299.0 27.9 reduce-scatter.14
  339.2 18.0 reduce-scatter.20
  365.3 22.7 all-gather.7
  391.6 28.0 reduce-scatter.22
  423.3 133.7 all-reduce.7
where the time goes:
time: 570 us; the launch traced here: 569 us
  waiting for transfers between devices  380 us (67%)
  blocking collectives  106 us (19%)
  matrix products  36.1 us (6%)
  other arithmetic  20.3 us (4%)
  between operations  14.8 us (3%)
  local copies, waits for them, and re-layouts  11.3 us (2%)
    psum x1, waiting for transfers between devices, body(): lax.psum((g_norm1_gain, g_norm1_bias, g_qkv_w, g_qv_b, g_out_w, g_out_b,...  108 us
    reduce_scatter x4, waiting for transfers between devices, narrow_sum(): lax.psum_scatter(partial_rows, 'width', scatter_dimension=1, tiled=True)  77.3 us
    psum x4, blocking collectives, moments(): return lax.psum((first_stat, second_stat), ('head', 'width'))  54.3 us
    all_gather x2, waiting for transfers between devices, hidden_whole(): return lax.all_gather(half_rows, 'head', axis=0, tiled=True)  52.5 us
    reduce_scatter x1, waiting for transfers between devices, body(): lax.psum_scatter(jnp.dot(picked, up_weight, preferred_element_type=jnp.fl...  45.7 us
    reduce_scatter x1, waiting for transfers between devices, body(): lax.psum_scatter(jnp.dot(picked, qkv_flat, preferred_element_type=jnp.flo...  34.6 us
    all_gather x4, blocking collectives, widen_rows(): return lax.all_gather(narrow_rows, 'width', axis=1, tiled=True)  31.1 us
    all_gather x1, waiting for transfers between devices, body(): grad_qkv_all = lax.all_gather(grad_qkv, 'head', axis=0, tiled=True)  22.9 us
  transfers between devices with their start and end apart: 12, of which 12 were waited for; matrix products, arithmetic and copies ran while one was open for 5% of the time, Pallas kernels for 0%

commit v1 on v0

--- a/solution.py
+++ b/solution.py
@@ -8,6 +8,22 @@
 norm_eps = 1e-05
 
 
+def gather_around(x, axis, dim):
+    ways, here, step = (lax.axis_size(axis), lax.axis_index(axis), x.shape[dim])
+    dims = [n * ways if d == dim else n for d, n in enumerate(x.shape)]
+    full = lax.dynamic_update_slice_in_dim(jnp.zeros(dims, x.dtype), x, here * step, axis=dim)
+    going_up = going_down = x
+    for far in range(1, ways // 2 + 1):
+        going_up = lax.ppermute(going_up, axis, [(d, (d + 1) % ways) for d in range(ways)])
+        full = lax.dynamic_update_slice_in_dim(full, going_up, (here - far) % ways * step, axis=dim)
+        if 2 * far < ways:
+            going_down = lax.ppermute(going_down, axis, [(d, (d - 1) % ways) for d in range(ways)])
+            full = lax.dynamic_update_slice_in_dim(
+                full, going_down, (here + far) % ways * step, axis=dim
+            )
+    return full
+
+
 def gelu_fn(values):
     return jax.nn.gelu(values, approximate=True)
 
@@ -17,7 +33,7 @@
 
 
 def widen_rows(narrow_rows):
-    return lax.all_gather(narrow_rows, "width", axis=1, tiled=True)
+    return gather_around(narrow_rows, "width", 1)
 
 
 def narrow_sum(partial_rows):

time: 570 us -> 575 us (level)
  blocking collectives: 106 us -> 74.5 us
  waiting for transfers between devices: 380 us -> 410 us
  starting transfers between devices: 0.67 us -> 7.67 us
    ppermute x0 -> x12, waiting for transfers between devices: none -> 37.5 us  [the longest x8 36.8 us: gather_around(): lax.ppermute(going_up, axis, [(d, (d + 1) % ways) for d in range(ways)])]
    all_gather x4 -> x0, blocking collectives: 31.1 us -> none  [widen_rows(): return lax.all_gather(narrow_rows, 'width', axis=1, tiled=True)]
    ppermute x0 -> x12, starting transfers between devices: none -> 7.17 us  [the longest x4 6.93 us: gather_around(): lax.ppermute(going_down, axis, [(d, (d - 1) % ways) for d in range(ways)])]
  transfers between devices with their start and end apart: 12 -> 24, of which waited for: 12 -> 21; matrix products, arithmetic and copies ran while one was open for 5% -> 5% of each run, Pallas kernels for 0% -> 0%
where the time goes in v1:
time: 575 us
  waiting for transfers between devices  410 us (71%)
  blocking collectives  74.5 us (13%)
  matrix products  36.1 us (6%)
  other arithmetic  20.4 us (4%)
  between operations  14.9 us (3%)
  local copies, waits for them, and re-layouts  11.4 us (2%)
  starting transfers between devices  7.67 us (1%)
    psum x1, waiting for transfers between devices, body(): lax.psum((g_norm1_gain, g_norm1_bias, g_qkv_w, g_qv_b, g_out_w, g_out_b,...  108 us
    reduce_scatter x4, waiting for transfers between devices, narrow_sum(): lax.psum_scatter(partial_rows, 'width', scatter_dimension=1, tiled=True)  74.5 us
    psum x4, blocking collectives, moments(): return lax.psum((first_stat, second_stat), ('head', 'width'))  54.3 us
    all_gather x2, waiting for transfers between devices, hidden_whole(): return lax.all_gather(half_rows, 'head', axis=0, tiled=True)  52.5 us
    reduce_scatter x1, waiting for transfers between devices, body(): lax.psum_scatter(jnp.dot(picked, up_weight, preferred_element_type=jnp.fl...  45.7 us
    ppermute x8, waiting for transfers between devices, gather_around(): lax.ppermute(going_up, axis, [(d, (d + 1) % ways) for d in range(ways)])  36.8 us
    reduce_scatter x1, waiting for transfers between devices, body(): lax.psum_scatter(jnp.dot(picked, qkv_flat, preferred_element_type=jnp.flo...  33.3 us
    all_gather x1, waiting for transfers between devices, body(): grad_qkv_all = lax.all_gather(grad_qkv, 'head', axis=0, tiled=True)  22.9 us
  transfers between devices with their start and end apart: 24, of which 21 were waited for; matrix products, arithmetic and copies ran while one was open for 5% of the time, Pallas kernels for 0%

profile of v1, /device:TPU:0, one launch (start us, length us, event | category | flops | bytes accessed | tf_op | source)
XLA Modules:
  0.0 574.7 jit_solution(16809205938326217497)
XLA Ops:
  8.4 15.4 %all-reduce.3 = (f32[1024]{0:T(1024)S(1)}, f32[1024]{0:T(1024)S(1)}) all-reduce(f32[1024]{0:T(1024)S(1)} %get-tuple-element.25, f32[1024]{0:T(1024)S(1)} %get-tuple-element.24), channel_id=1, replica_groups=mesh['dp'=4,'head'=2,'width'=4] {'head','width'}, use_global_device_ids=true, to_apply=%region_3.0 | all-reduce | flops 2048 | bytes 16384 | tf_op jit(solution)/shard_map/psum | solution.py:32
  26.8 4.6 collective-permute-done
  31.4 5.0 collective-permute-done.2
  39.8 33.3 %reduce-scatter.9.cloned.1.call-done = f32[512,576]{0,1:T(8,128)} async-done(((f32[1024,576]{0,1:T(8,128)}), f32[512,576]{0,1:T(8,128)}) %reduce-scatter.9.cloned.1.call-update) | async-done | bytes 1179664 | tf_op jit(solution)/shard_map/reduce_scatter | solution.py:90
  78.9 7.2 %all_gather.12 = bf16[1024,192]{0,1:T(8,128)(2,1)S(1)} all-gather(bf16[512,192]{0,1:T(8,128)(2,1)S(1)} %bitcast.65), channel_id=1, replica_groups=mesh['dp'=4,'head'=2,'width'=4] {'head'}, dimensions={0}, use_global_device_ids=true | all-gather | bytes 589824 | tf_op jit(solution)/shard_map/all_gather | solution.py:118
  90.4 3.7 collective-permute-done.6
  94.8 4.4 collective-permute-done.8
  102.0 13.7 %reduce-scatter.11.cloned.1.call-done = f32[1024,96]{0,1:T(8,128)} async-done(((f32[1024,384]{0,1:T(8,128)}), f32[1024,96]{0,1:T(8,128)}) %reduce-scatter.11.cloned.1.call-update) | async-done | bytes 393232 | tf_op jit(solution)/shard_map/reduce_scatter | solution.py:40
  116.9 13.3 %all-reduce.2 = (f32[1024]{0:T(1024)S(1)}, f32[1024]{0:T(1024)S(1)}) all-reduce(f32[1024]{0:T(1024)S(1)} %get-tuple-element.23, f32[1024]{0:T(1024)S(1)} %get-tuple-element.22), channel_id=1, replica_groups=mesh['dp'=4,'head'=2,'width'=4] {'head','width'}, use_global_device_ids=true, to_apply=%region_11.12 | all-reduce | flops 2048 | bytes 16384 | tf_op jit(solution)/shard_map/psum | solution.py:32
  132.4 4.2 collective-permute-done.3
  136.7 5.0 collective-permute-done.5
  144.5 17.1 %reduce-scatter.17.cloned.1.call-done = f32[512,768]{1,0:T(8,128)} async-done(((f32[1024,768]{1,0:T(8,128)}), f32[512,768]{1,0:T(8,128)}) %reduce-scatter.17.cloned.1.call-update) | async-done | bytes 1572880 | tf_op jit(solution)/shard_map/reduce_scatter | solution.py:160
  161.6 45.7 %reduce-scatter.13.cloned.1.call-done = f32[512,768]{1,0:T(8,128)} async-done(((f32[1024,768]{1,0:T(8,128)}), f32[512,768]{1,0:T(8,128)}) %reduce-scatter.13.cloned.1.call-update) | async-done | bytes 1572880 | tf_op jit(solution)/shard_map/reduce_scatter | solution.py:128
  207.2 4.2 fusion.8
  212.1 26.7 %all-gather.6.cloned.1.call-done = bf16[1024,768]{1,0:T(8,128)(2,1)} async-done(((bf16[512,768]{1,0:T(8,128)(2,1)}), bf16[1024,768]{1,0:T(8,128)(2,1)}) %all-gather.6.cloned.1.call-update) | async-done | bytes 1572880 | tf_op jit(solution)/shard_map/all_gather | solution.py:44
  238.8 3.4 fusion.54
  242.2 25.8 %all-gather.4.cloned.1.call-done = bf16[1024,768]{1,0:T(8,128)(2,1)} async-done(((bf16[512,768]{1,0:T(8,128)(2,1)}), bf16[1024,768]{1,0:T(8,128)(2,1)}) %all-gather.4.cloned.1.call-update) | async-done | bytes 1572880 | tf_op jit(solution)/shard_map/all_gather | solution.py:44
  268.0 3.6 fusion.52
  271.6 26.9 %reduce-scatter.19.cloned.1.call-done = f32[1024,96]{0,1:T(8,128)} async-done(((f32[1024,384]{0,1:T(8,128)}), f32[1024,96]{0,1:T(8,128)}) %reduce-scatter.19.cloned.1.call-update) | async-done | bytes 393232 | tf_op jit(solution)/shard_map/reduce_scatter | solution.py:40
  300.3 12.7 %all-reduce.1 = (f32[1024]{0:T(1024)S(1)}, f32[1024]{0:T(1024)S(1)}) all-reduce(f32[1024]{0:T(1024)S(1)} %get-tuple-element.15, f32[1024]{0:T(1024)S(1)} %get-tuple-element.19), channel_id=1, replica_groups=mesh['dp'=4,'head'=2,'width'=4] {'head','width'}, use_global_device_ids=true, to_apply=%region_20.21 | all-reduce | flops 2048 | bytes 16384 | tf_op jit(solution)/shard_map/psum | solution.py:32
  313.1 16.1 %reduce-scatter.15.cloned.1.call-done = f32[1024,96]{0,1:T(8,128)} async-done(((f32[1024,384]{0,1:T(8,128)}), f32[1024,96]{0,1:T(8,128)}) %reduce-scatter.15.cloned.1.call-update) | async-done | bytes 393232 | tf_op jit(solution)/shard_map/reduce_scatter | solution.py:40
  333.7 4.8 collective-permute-done.9
  338.6 5.0 collective-permute-done.11
  345.0 17.4 %reduce-scatter.21.cloned.1.call-done = f32[512,192]{0,1:T(8,128)} async-done(((f32[1024,192]{0,1:T(8,128)}), f32[512,192]{0,1:T(8,128)}) %reduce-scatter.21.cloned.1.call-update) | async-done | bytes 393232 | tf_op jit(solution)/shard_map/reduce_scatter | solution.py:181
  363.5 3.4 multiply_convert_fusion
  371.0 22.9 %all-gather.8.cloned.1.call-done = bf16[1024,576]{0,1:T(8,128)(2,1)} async-done(((bf16[512,576]{0,1:T(8,128)(2,1)}), bf16[1024,576]{0,1:T(8,128)(2,1)}) %all-gather.8.cloned.1.call-update) | async-done | bytes 1179664 | tf_op jit(solution)/shard_map/all_gather | solution.py:208
  393.8 3.3 fusion.55
  397.3 3.3 fusion.58
  407.7 17.7 %reduce-scatter.23.cloned.1.call-done = f32[1024,96]{0,1:T(8,128)} async-done(((f32[1024,384]{0,1:T(8,128)}), f32[1024,96]{0,1:T(8,128)}) %reduce-scatter.23.cloned.1.call-update) | async-done | bytes 393232 | tf_op jit(solution)/shard_map/reduce_scatter | solution.py:40
  426.7 13.0 %all-reduce.4 = (f32[96]{0:T(128)}, f32[96]{0:T(128)}, f32[2,192]{1,0:T(2,128)}, f32[96]{0:T(128)}, f32[96]{0:T(128)}, /*index=5*/f32[96]{0:T(128)}, f32[768]{0:T(1024)}, f32[96]{0:T(128)}) all-reduce(f32[96]{0:T(128)S(1)} %get-tuple-element.16, f32[96]{0:T(128)S(1)} %get-tuple-element.21, ...), channel_id=1, replica_groups=mesh['dp'=4,'head'=2,'width'=4] {'dp'}, use_global_device_ids=true, to_apply=%region_29.30 | all-reduce | flops 1728 | bytes 13824 | tf_op jit(solution)/shard_map/psum | solution.py:220
  439.7 12.8 %all-reduce = (f32[1024]{0:T(1024)S(1)}, f32[1024]{0:T(1024)S(1)}) all-reduce(f32[1024]{0:T(1024)S(1)} %get-tuple-element.17, f32[1024]{0:T(1024)S(1)} %get-tuple-element.18), channel_id=1, replica_groups=mesh['dp'=4,'head'=2,'width'=4] {'head','width'}, use_global_device_ids=true, to_apply=%region_27.28 | all-reduce | flops 2048 | bytes 16384 | tf_op jit(solution)/shard_map/psum | solution.py:32
  454.4 108.4 %all-reduce.8.cloned.1.call-done = (f32[384,3,192]{0,2,1:T(8,128)}, f32[192,384]{1,0:T(8,128)}, f32[384,768]{1,0:T(8,128)}, f32[768,384]{1,0:T(8,128)}) async-done(((f32[384,3,192]{0,2,1:T(8,128)}, f32[192,384]{1,0:T(8,128)}, f32[384,768]{1,0:T(8,128)}, f32[768,384]{1,0:T(8,128)}), (f32[384,3,192]{0,2,1:T(8,128)}, f32[192,384]{1,0:T(8,128)}, f32[384,768]{1,0:T(8,128)}, ...) | async-done | bytes 3538960 | tf_op jit(solution)/shard_map/psum | solution.py:220
  (185 shorter events, 55.7 us)
Async XLA Ops:
  7.2 134.5 %copy-start = (bf16[384,768]{1,0:T(8,128)(2,1)S(1)}, bf16[384,768]{1,0:T(8,128)(2,1)}, u32[]{:S(2)}) copy-start(bf16[384,768]{1,0:T(8,128)(2,1)} %param.27) | copy-start | bytes 1769476
  7.2 29.3 %copy-start.14 = (bf16[384,3,192]{0,2,1:T(8,128)(2,1)S(1)}, bf16[384,3,192]{0,2,1:T(8,128)(2,1)}, u32[]{:S(2)}) copy-start(bf16[384,3,192]{0,2,1:T(8,128)(2,1)} %param.21) | copy-start | bytes 1327108
  7.2 65.9 %reduce-scatter.9.cloned.1.call-start = ((), (), s32[]{:S(2)}) async-start(), calls=%async_computation.8 | async-start | bytes 3538944 | tf_op jit(solution)/shard_map/reduce_scatter | solution.py:90
  25.0 6.4 %collective-permute-start = (bf16[1024,96]{0,1:T(8,128)(2,1)S(1)}, bf16[1024,96]{0,1:T(8,128)(2,1)S(1)}, u32[]{:S(2)}, u32[]{:S(2)}) collective-permute-start(bf16[1024,96]{0,1:T(8,128)(2,1)S(1)} %get-tuple-element.58), channel_id=1, source_target_pairs={{0,1},{1,2},{2,3},{3,0},{4,5},{5,6},{6,7},{7,4},{8,9},{9,10},{10,1... | collective-permute-start | bytes 589832 | tf_op jit(solution)/shard_map/ppermute | solution.py:17
  25.1 6.3 %collective-permute-start.1 = (bf16[1024,96]{0,1:T(8,128)(2,1)S(1)}, bf16[1024,96]{0,1:T(8,128)(2,1)S(1)}, u32[]{:S(2)}, u32[]{:S(2)}) collective-permute-start(bf16[1024,96]{0,1:T(8,128)(2,1)S(1)} %get-tuple-element.58), channel_id=1, source_target_pairs={{0,3},{1,0},{2,1},{3,2},{4,7},{5,4},{6,5},{7,6},{8,11},{9,8},{10,9... | collective-permute-start | bytes 589832 | tf_op jit(solution)/shard_map/ppermute | solution.py:20
  31.4 5.1 collective-permute-start.2
  38.7 77.0 %reduce-scatter.11.cloned.1.call-start = ((), (), s32[]{:S(2)}) async-start(), calls=%async_computation.9 | async-start | bytes 1966080 | tf_op jit(solution)/shard_map/reduce_scatter | solution.py:40
  39.8 37.2 %copy-start.10 = (pred[512,512]{0,1:T(8,128)(4,1)}, pred[512,512]{0,1:T(8,128)(4,1)S(1)}, u32[]{:S(2)}) copy-start(pred[512,512]{0,1:T(8,128)(4,1)S(1)} %fusion.14) | copy-start | bytes 786436
  87.7 73.9 %reduce-scatter.17.cloned.1.call-start = ((), (), s32[]{:S(2)}) async-start(), calls=%async_computation.13 | async-start | bytes 4718592 | tf_op jit(solution)/shard_map/reduce_scatter | solution.py:160
  88.6 5.5 collective-permute-start.6
  88.7 6.2 %collective-permute-start.7 = (bf16[1024,96]{0,1:T(8,128)(2,1)S(1)}, bf16[1024,96]{0,1:T(8,128)(2,1)S(1)}, u32[]{:S(2)}, u32[]{:S(2)}) collective-permute-start(bf16[1024,96]{0,1:T(8,128)(2,1)S(1)} %get-tuple-element.53), channel_id=1, source_target_pairs={{0,3},{1,0},{2,1},{3,2},{4,7},{5,4},{6,5},{7,6},{8,11},{9,8},{10,9... | collective-permute-start | bytes 589832 | tf_op jit(solution)/shard_map/ppermute | solution.py:20
  94.1 5.1 collective-permute-start.8
  102.0 28.4 %copy-start.29 = (f32[96]{0:T(128)S(1)}, f32[96]{0:T(128)}, u32[]{:S(2)}) copy-start(f32[96]{0:T(128)} %param.25) | copy-start | bytes 1156
  102.0 28.4 %copy-start.38 = (f32[96]{0:T(128)S(1)}, f32[96]{0:T(128)}, u32[]{:S(2)}) copy-start(f32[96]{0:T(128)} %param.26) | copy-start | bytes 1156
  102.0 105.2 %reduce-scatter.13.cloned.1.call-start = ((), (), s32[]{:S(2)}) async-start(), calls=%async_computation.10 | async-start | bytes 4718592 | tf_op jit(solution)/shard_map/reduce_scatter | solution.py:128
  130.6 6.0 %collective-permute-start.3 = (bf16[1024,96]{0,1:T(8,128)(2,1)S(1)}, bf16[1024,96]{0,1:T(8,128)(2,1)S(1)}, u32[]{:S(2)}, u32[]{:S(2)}) collective-permute-start(bf16[1024,96]{0,1:T(8,128)(2,1)S(1)} %get-tuple-element.55), channel_id=1, source_target_pairs={{0,1},{1,2},{2,3},{3,0},{4,5},{5,6},{6,7},{7,4},{8,9},{9,10},{10,1... | collective-permute-start | bytes 589832 | tf_op jit(solution)/shard_map/ppermute | solution.py:17
  130.6 6.0 %collective-permute-start.4 = (bf16[1024,96]{0,1:T(8,128)(2,1)S(1)}, bf16[1024,96]{0,1:T(8,128)(2,1)S(1)}, u32[]{:S(2)}, u32[]{:S(2)}) collective-permute-start(bf16[1024,96]{0,1:T(8,128)(2,1)S(1)} %get-tuple-element.55), channel_id=1, source_target_pairs={{0,3},{1,0},{2,1},{3,2},{4,7},{5,4},{6,5},{7,6},{8,11},{9,8},{10,9... | collective-permute-start | bytes 589832 | tf_op jit(solution)/shard_map/ppermute | solution.py:20
  136.6 5.1 collective-permute-start.5
  144.4 62.8 %copy-start.30 = (f32[768]{0:T(1024)S(1)}, f32[768]{0:T(1024)}, u32[]{:S(2)}) copy-start(f32[768]{0:T(1024)} %param.28) | copy-start | bytes 9220
  144.5 94.3 %all-gather.6.cloned.1.call-start = ((), (), s32[]{:S(2)}) async-start(), calls=%async_computation.14 | async-start | bytes 2359296 | tf_op jit(solution)/shard_map/all_gather | solution.py:44
  211.5 56.5 %all-gather.4.cloned.1.call-start = ((), (), s32[]{:S(2)}) async-start(), calls=%async_computation.11 | async-start | bytes 2359296 | tf_op jit(solution)/shard_map/all_gather | solution.py:44
  212.0 86.5 %reduce-scatter.19.cloned.1.call-start = ((), (), s32[]{:S(2)}) async-start(), calls=%async_computation.15 | async-start | bytes 1966080 | tf_op jit(solution)/shard_map/reduce_scatter | solution.py:40
  242.2 87.0 %reduce-scatter.15.cloned.1.call-start = ((), (), s32[]{:S(2)}) async-start(), calls=%async_computation.12 | async-start | bytes 1966080 | tf_op jit(solution)/shard_map/reduce_scatter | solution.py:40
  271.6 57.6 %copy-start.39 = (f32[96]{0:T(128)S(1)}, f32[96]{0:T(128)}, u32[]{:S(2)}) copy-start(f32[96]{0:T(128)} %param.30) | copy-start | bytes 1156
  271.6 90.8 %reduce-scatter.21.cloned.1.call-start = ((), (), s32[]{:S(2)}) async-start(), calls=%async_computation.16 | async-start | bytes 1179648 | tf_op jit(solution)/shard_map/reduce_scatter | solution.py:181
  331.9 6.6 %collective-permute-start.9 = (bf16[1024,96]{0,1:T(8,128)(2,1)S(1)}, bf16[1024,96]{0,1:T(8,128)(2,1)S(1)}, u32[]{:S(2)}, u32[]{:S(2)}) collective-permute-start(bf16[1024,96]{0,1:T(8,128)(2,1)S(1)} %get-tuple-element.51), channel_id=1, source_target_pairs={{0,1},{1,2},{2,3},{3,0},{4,5},{5,6},{6,7},{7,4},{8,9},{9,10},{10,1... | collective-permute-start | bytes 589832 | tf_op jit(solution)/shard_map/ppermute | solution.py:17
  332.0 6.6 %collective-permute-start.10 = (bf16[1024,96]{0,1:T(8,128)(2,1)S(1)}, bf16[1024,96]{0,1:T(8,128)(2,1)S(1)}, u32[]{:S(2)}, u32[]{:S(2)}) collective-permute-start(bf16[1024,96]{0,1:T(8,128)(2,1)S(1)} %get-tuple-element.51), channel_id=1, source_target_pairs={{0,3},{1,0},{2,1},{3,2},{4,7},{5,4},{6,5},{7,6},{8,11},{9,8},{10,9... | collective-permute-start | bytes 589832 | tf_op jit(solution)/shard_map/ppermute | solution.py:20
  338.5 5.1 collective-permute-start.11
  344.9 48.9 %all-gather.8.cloned.1.call-start = ((), (), s32[]{:S(2)}) async-start(), calls=%async_computation.17 | async-start | bytes 1769472 | tf_op jit(solution)/shard_map/all_gather | solution.py:208
  370.9 54.5 %reduce-scatter.23.cloned.1.call-start = ((), (), s32[]{:S(2)}) async-start(), calls=%async_computation.18 | async-start | bytes 1966080 | tf_op jit(solution)/shard_map/reduce_scatter | solution.py:40
  397.2 165.6 %all-reduce.8.cloned.1.call-start = ((), (), s32[]{:S(2)}) async-start(), calls=%async_computation.19 | async-start | bytes 7077888 | tf_op jit(solution)/shard_map/psum | solution.py:220
  405.6 21.1 %copy-start.32 = (f32[96]{0:T(128)S(1)}, f32[96]{0:T(128)}, u32[]{:S(2)}) copy-start(f32[96]{0:T(128)} %get-tuple-element.14) | copy-start | bytes 1156
  (32 other events, 197.7 us)
Sparse Core Ops, SparseCore 0:
  38.9 34.1 reduce-scatter.8
  87.8 27.9 reduce-scatter.10
  118.0 43.5 reduce-scatter.16
  163.7 43.5 reduce-scatter.12
  211.6 27.1 all-gather.5
  240.8 27.1 all-gather.3
  270.5 28.0 reduce-scatter.18
  301.1 27.9 reduce-scatter.14
  345.0 17.2 reduce-scatter.20
  371.1 22.7 all-gather.7
  397.3 28.0 reduce-scatter.22
  429.1 133.7 all-reduce.7
